TPU v7x, 1024 devices: a whole 4x8x16 slice. The times are simulated.
1024 devices in a mesh: sub: 64 (over z, x), grp: 16 (over y, core).
Axes of the slice: x: 4, y: 8, z: 16, core: 2. Of those that a mesh axis runs over, the one named last changes fastest.
Arguments:
- flexibility: bfloat16 [64, 16, 512, 512], P('sub', 'grp'), as said below
- dirichlet_schur: bfloat16 [64, 16, 512, 512], P('sub', 'grp'), as said below
- subdomain_loads: bfloat16 [64, 16, 512, 128], P('sub', 'grp'), may hold values from -6 to 6
- coupling: bfloat16 [64, 16, 512, 24], P('sub', 'grp'), may hold values from -0.25 to 0.25
- coarse_rows: bfloat16 [64, 16, 24, 2048], P('sub', 'grp'), as said below
- neighbors: int32 [64, 16, 28], P('sub', 'grp'), may hold values from 0 to 63, as said below
- interface_rows: int32 [64, 16, 28, 16], P('sub', 'grp'), may hold values from 0 to 511, as said below
- coarse_map: int32 [64, 16, 24], P('sub', 'grp'), may hold values from 0 to 2047, as said below
Outputs:
- solution: float32 [64, 16, 512, 128], P('sub', 'grp')
- preconditioned: float32 [64, 16, 512, 128], P('sub', 'grp')
Inputs may be any that keep to these rules, and one draw needn't show every extreme that they name: `neighbors`: each subdomain lists 28 distinct sub indices other than its own, of subdomains with the same grp index; if subdomain (i, g) lists j, then (j, g) lists i. `interface_rows`: the 28 x 16 rows of one subdomain are distinct; the j-th row that s lists for neighbor t and the j-th row that t lists for s are the same interface point. `coarse_map`: the 24 entries of one subdomain are distinct. coarse_rows of subdomain s are the rows coarse_map of s of one symmetric positive definite matrix of order 2048. `flexibility`: each subdomain's block is symmetric positive definite. `dirichlet_schur`: each subdomain's block is symmetric positive definite.
All inputs are finite; a program needn't handle non-finite values.
Results may differ from a plain program's by a relative error of at most 0.0084.
Values may be sent and summed in bfloat16 or wider, within the bound.
A program may use at most 32 MiB of HBM per device.

v0:
```python
import jax
import jax.numpy as jnp
from jax import lax
from jax.sharding import PartitionSpec as P


def body(
    flexibility,
    dirichlet_schur,
    subdomain_loads,
    coupling,
    coarse_rows,
    neighbors,
    interface_rows,
    coarse_map,
):
    flex_block = flexibility[0, 0]
    schur_block = dirichlet_schur[0, 0]
    loads_block = subdomain_loads[0, 0]
    couple_block = coupling[0, 0]
    coarse_block = coarse_rows[0, 0]
    neighbor_ids = neighbors[0, 0]
    row_lists = interface_rows[0, 0]
    corner_ids = coarse_map[0, 0]
    order_size = flex_block.shape[0]
    column_count = loads_block.shape[1]
    coarse_size = coarse_block.shape[1]
    line_size = lax.axis_size("sub")
    flat_rows = row_lists.reshape(-1)
    destinations = (
        jnp.arange(line_size, dtype=jnp.int32)[:, None] == neighbor_ids[None, :]
    ).astype(jnp.bfloat16)
    pair_mask = jnp.zeros((order_size,), jnp.float32).at[flat_rows].set(1.0)
    weight = (1.0 - 0.5 * pair_mask)[:, None]

    def jump_field(surface):
        picked = surface[flat_rows].reshape(row_lists.shape + (column_count,))
        outgoing = jnp.einsum(
            "dk,kjc->djc", destinations, picked, preferred_element_type=jnp.float32
        ).astype(jnp.bfloat16)
        incoming = lax.all_to_all(outgoing, "sub", split_axis=0, concat_axis=0, tiled=True)
        matched = jnp.einsum(
            "dk,djc->kjc", destinations, incoming, preferred_element_type=jnp.float32
        )
        placed = (
            jnp.zeros((order_size, column_count), jnp.float32)
            .at[flat_rows]
            .set(matched.reshape(-1, column_count))
        )
        return surface.astype(jnp.float32) - placed

    def precondition(residual):
        scaled = (weight * residual).astype(jnp.bfloat16)
        schur_image = jnp.dot(schur_block, scaled, preferred_element_type=jnp.float32).astype(
            jnp.bfloat16
        )
        return weight * jump_field(schur_image)

    def column_dot(first_field, second_field):
        return lax.psum(jnp.sum(weight * first_field * second_field, axis=0), ("sub", "grp"))

    residual = jump_field(loads_block)
    zfield = precondition(residual)
    direction = zfield
    inner = column_dot(residual, zfield)
    dir_half = direction.astype(jnp.bfloat16)
    local_part = jnp.dot(flex_block, dir_half, preferred_element_type=jnp.float32)
    coarse_in = jnp.dot(couple_block.T, dir_half, preferred_element_type=jnp.float32)
    dense_sum = jnp.zeros((coarse_size, column_count), jnp.float32).at[corner_ids].set(coarse_in)
    partial_rows = lax.psum_scatter(dense_sum, "sub", scatter_dimension=0, tiled=True)
    panel_half = lax.psum(partial_rows, "grp").astype(jnp.bfloat16)
    coarse_val = jnp.dot(
        coarse_block,
        lax.all_gather(panel_half, "sub", axis=0, tiled=True),
        preferred_element_type=jnp.float32,
    ).astype(jnp.bfloat16)
    surface = (
        local_part + jnp.dot(couple_block, coarse_val, preferred_element_type=jnp.float32)
    ).astype(jnp.bfloat16)
    operated = jump_field(surface)
    step_size = inner / column_dot(direction, operated)
    solution = step_size * direction
    residual = residual - step_size * operated
    zfield = precondition(residual)
    return (solution[None, None], zfield[None, None])


def solution(mesh):
    placed = (
        P("sub", "grp", None, None),
        P("sub", "grp", None, None),
        P("sub", "grp", None, None),
        P("sub", "grp", None, None),
        P("sub", "grp", None, None),
        P("sub", "grp", None),
        P("sub", "grp", None, None),
        P("sub", "grp", None),
    )
    return jax.shard_map(
        body,
        mesh=mesh,
        in_specs=placed,
        out_specs=(P("sub", "grp", None, None), P("sub", "grp", None, None)),
        check_vma=False,
    )
```

profile of v0, /device:TPU:1, one launch (start us, length us, event | category | flops | bytes accessed | tf_op | source)
XLA Modules:
  0.0 1128.0 jit_solution(15750849499144985489)
XLA Ops:
  7.2 0.8 copy.36
  8.1 2.1 gather_fusion
  10.3 0.6 copy-done.5
  10.9 0.3 convolution_convert_fusion.3
  11.3 0.9 copy.40
  12.1 22.9 %all-to-all-start = ((bf16[64,16,128]{2,1,0:T(8,128)(2,1)}), bf16[64,16,128]{2,1,0:T(8,128)(2,1)S(1)}, u32[]{:S(2)}, u32[]{:S(2)}) async-start(bf16[64,16,128]{2,1,0:T(8,128)(2,1)} %copy.40), calls=%async_computation | async-start | bytes 524288 | tf_op jit(solution)/shard_map/all_to_all | solution.py:41
  35.2 2.9 scatter_custom_fusion
  38.1 16.4 %all-to-all-done = bf16[64,16,128]{2,1,0:T(8,128)(2,1)S(1)} async-done(((bf16[64,16,128]{2,1,0:T(8,128)(2,1)}), bf16[64,16,128]{2,1,0:T(8,128)(2,1)S(1)}, u32[]{:S(2)}, u32[]{:S(2)}) %all-to-all-start) | async-done | bytes 262176 | tf_op jit(solution)/shard_map/all_to_all | solution.py:41
  54.5 0.2 fusion.16
  54.8 0.1 copy.42
  54.9 1.6 scatter_custom_fusion.1
  56.7 0.3 fusion.1
  57.2 1.5 gather_fusion.1
  58.6 0.3 convolution_convert_fusion.2
  59.0 0.9 copy.46
  59.9 7.2 all-to-all-start.1
  67.1 18.5 %all-to-all-done.1 = bf16[64,16,128]{2,1,0:T(8,128)(2,1)S(1)} async-done(((bf16[64,16,128]{2,1,0:T(8,128)(2,1)}), bf16[64,16,128]{2,1,0:T(8,128)(2,1)S(1)}, u32[]{:S(2)}, u32[]{:S(2)}) %all-to-all-start.1) | async-done | bytes 262176 | tf_op jit(solution)/shard_map/all_to_all | solution.py:41
  85.7 0.2 fusion.14
  85.9 0.1 copy.48
  86.0 1.6 scatter_custom_fusion.2
  87.9 0.7 copy-done.4
  88.7 1.7 scatter_custom_fusion.3
  90.4 688.5 %reduce-scatter.2.cloned.1.call-done = f32[32,128]{1,0:T(8,128)} async-done(((f32[2048,128]{1,0:T(8,128)}), f32[32,128]{1,0:T(8,128)}) %reduce-scatter.2.cloned.1.call-update) | async-done | bytes 16400 | tf_op jit(solution)/shard_map/reduce_scatter | solution.py:70
  778.9 54.4 %psum.22 = bf16[32,128]{1,0:T(8,128)(2,1)S(1)} all-reduce(f32[32,128]{1,0:T(8,128)} %reduce-scatter.2.cloned.1.call-done), channel_id=1, replica_groups=mesh['sub'=64,'grp'=16] {'grp'}, use_global_device_ids=true, to_apply=%region_7.0 | all-reduce | flops 4096 | bytes 24576 | tf_op jit(solution)/shard_map/psum | solution.py:71
  833.3 72.5 %all_gather.3 = bf16[2048,128]{1,0:T(8,128)(2,1)S(1)} all-gather(bf16[32,128]{1,0:T(8,128)(2,1)S(1)} %psum.22), channel_id=1, replica_groups=mesh['sub'=64,'grp'=16] {'sub'}, dimensions={0}, use_global_device_ids=true | all-gather | bytes 532480 | tf_op jit(solution)/shard_map/all_gather | solution.py:74
  905.8 0.4 fusion.4
  906.3 0.6 copy-done.2
  906.9 0.3 fusion.3
  907.3 1.5 gather_fusion.2
  908.8 0.3 convolution_convert_fusion.1
  909.2 0.2 copy.52
  909.4 28.5 %all_to_all.20 = bf16[64,16,128]{2,1,0:T(8,128)(2,1)S(1)} all-to-all(bf16[64,16,128]{2,1,0:T(8,128)(2,1)S(1)} %copy.52), channel_id=1, replica_groups=mesh['sub'=64,'grp'=16] {'sub'}, dimensions={0} | all-to-all | bytes 524288 | tf_op jit(solution)/shard_map/all_to_all | solution.py:41
  937.9 0.2 fusion.12
  938.1 0.1 copy.54
  938.3 1.6 scatter_custom_fusion.4
  940.1 0.2 multiply_reduce_fusion
  940.2 147.9 %all-reduce = (f32[128]{0:T(128)S(1)}, f32[128]{0:T(128)S(1)}) all-reduce(f32[128]{0:T(128)S(1)} %get-tuple-element.9, f32[128]{0:T(128)S(1)} %get-tuple-element.8), channel_id=1, replica_groups=mesh['sub'=64,'grp'=16] {'sub','grp'}, use_global_device_ids=true, to_apply=%region_4.0 | all-reduce | flops 256 | bytes 2048 | tf_op jit(solution)/shard_map/psum | solution.py:60
  1088.1 0.3 fusion.2
  1088.6 1.5 gather_fusion.3
  1090.1 0.3 convolution_convert_fusion
  1090.4 0.9 copy.58
  1091.3 7.3 all-to-all-start.3
  1098.7 0.8 copy.62
  1099.6 18.6 %all-to-all-done.3 = bf16[64,16,128]{2,1,0:T(8,128)(2,1)S(1)} async-done(((bf16[64,16,128]{2,1,0:T(8,128)(2,1)}), bf16[64,16,128]{2,1,0:T(8,128)(2,1)S(1)}, u32[]{:S(2)}, u32[]{:S(2)}) %all-to-all-start.3) | async-done | bytes 262176 | tf_op jit(solution)/shard_map/all_to_all | solution.py:41
  1118.1 0.2 fusion.10
  1118.4 0.1 copy.60
  1118.5 1.6 scatter_custom_fusion.5
  1120.3 0.8 copy.63
  (32 shorter events, 1.5 us)
Async XLA Ops:
  7.2 49.5 %copy-start = (bf16[1,1,512,512]{3,2,1,0:T(8,128)(2,1)S(1)}, bf16[1,1,512,512]{3,2,1,0:T(8,128)(2,1)}, u32[]{:S(2)}) copy-start(bf16[1,1,512,512]{3,2,1,0:T(8,128)(2,1)} %param.9) | copy-start | bytes 1572868
  10.3 0.7 copy-start.5
  12.1 22.9 %copy-start.1 = (bf16[1,1,512,128]{3,2,1,0:T(8,128)(2,1)S(1)}, bf16[1,1,512,128]{3,2,1,0:T(8,128)(2,1)}, u32[]{:S(2)}) copy-start(bf16[1,1,512,128]{3,2,1,0:T(8,128)(2,1)} %param.10) | copy-start | bytes 393220
  12.1 42.4 %all-to-all-start = ((bf16[64,16,128]{2,1,0:T(8,128)(2,1)}), bf16[64,16,128]{2,1,0:T(8,128)(2,1)S(1)}, u32[]{:S(2)}, u32[]{:S(2)}) async-start(bf16[64,16,128]{2,1,0:T(8,128)(2,1)} %copy.40), calls=%async_computation | async-start | bytes 524288 | tf_op jit(solution)/shard_map/all_to_all | solution.py:41
  59.9 7.2 copy-start.6
  59.9 25.8 %all-to-all-start.1 = ((bf16[64,16,128]{2,1,0:T(8,128)(2,1)}), bf16[64,16,128]{2,1,0:T(8,128)(2,1)S(1)}, u32[]{:S(2)}, u32[]{:S(2)}) async-start(bf16[64,16,128]{2,1,0:T(8,128)(2,1)} %copy.46), calls=%async_computation.1 | async-start | bytes 524288 | tf_op jit(solution)/shard_map/all_to_all | solution.py:41
  67.1 711.8 %reduce-scatter.2.cloned.1.call-start = ((), (), s32[]{:S(2)}) async-start(), calls=%async_computation.5 | async-start | bytes 1064960 | tf_op jit(solution)/shard_map/reduce_scatter | solution.py:70
  87.8 0.7 copy-start.4
  833.3 72.5 %copy-start.3 = (bf16[1,1,24,2048]{3,2,1,0:T(8,128)(2,1)S(1)}, bf16[1,1,24,2048]{3,2,1,0:T(8,128)(2,1)}, u32[]{:S(2)}) copy-start(bf16[1,1,24,2048]{3,2,1,0:T(8,128)(2,1)} %param.12) | copy-start | bytes 294916
  905.8 1.0 copy-start.2
  1091.3 26.8 %all-to-all-start.3 = ((bf16[64,16,128]{2,1,0:T(8,128)(2,1)}), bf16[64,16,128]{2,1,0:T(8,128)(2,1)S(1)}, u32[]{:S(2)}, u32[]{:S(2)}) async-start(bf16[64,16,128]{2,1,0:T(8,128)(2,1)} %copy.58), calls=%async_computation.4 | async-start | bytes 524288 | tf_op jit(solution)/shard_map/all_to_all | solution.py:41
Sparse Core Ops, SparseCore 0:
  90.5 688.3 reduce-scatter.1
where the time goes:
time: 1130 us
  waiting for transfers between devices  742 us (66%)
  blocking collectives  303 us (27%)
  starting transfers between devices  37.4 us (3%)
  local copies, waits for them, and re-layouts  26.7 us (2%)
  between operations  14.4 us (1%)
    reduce_scatter x1, waiting for transfers between devices, body(): lax.psum_scatter(dense_sum, 'sub', scatter_dimension=0, tiled=True)  688 us
    psum x1, blocking collectives, column_dot(): lax.psum(jnp.sum(weight * first_field * second_field, axis=0), ('sub', 'g...  148 us
    all_gather x1, blocking collectives, body(): lax.all_gather(panel_half, 'sub', axis=0, tiled=True)  72.5 us
    psum x1, blocking collectives, body(): panel_half = lax.psum(partial_rows, 'grp').astype(jnp.bfloat16)  54.4 us
    all_to_all x3, waiting for transfers between devices, jump_field(): lax.all_to_all(outgoing, 'sub', split_axis=0, concat_axis=0, tiled=True)  53.5 us
    all_to_all x3, starting transfers between devices, jump_field(): lax.all_to_all(outgoing, 'sub', split_axis=0, concat_axis=0, tiled=True)  37.4 us
    all_to_all x1, blocking collectives, jump_field(): lax.all_to_all(outgoing, 'sub', split_axis=0, concat_axis=0, tiled=True)  28.5 us
  transfers between devices with their start and end apart: 4, of which 4 were waited for; matrix products, arithmetic and copies ran while one was open for 0% of the time, Pallas kernels for 0%

commit v1 on v0

v1 whole, which is shorter than its diff:
```python
import functools

import jax
import jax.numpy as jnp
from jax import lax
from jax.experimental import pallas as pl
from jax.experimental.pallas import tpu as pltpu
from jax.sharding import PartitionSpec as P

F32 = jnp.float32
BF16 = jnp.bfloat16
MESH = pl.DeviceIdType.MESH
CORNER_PAD = 32


def dot(a, b):
    return jnp.dot(a, b, preferred_element_type=F32)


def kernel(
    x_size,
    flex_ref,
    schur_ref,
    loads_ref,
    couple_ref,
    coarse_ref,
    slot_col_ref,
    slot_row_ref,
    map_ref,
    solution_ref,
    precond_ref,
    pick,
    place,
    jump_out,
    jump_in,
    map_out,
    map_in,
    rows_out,
    rows_in,
    corner_out,
    corner_in,
    zsum_out,
    zsum_in,
    xsum_out,
    xsum_in,
    gather_out,
    gather_in,
    val_out,
    val_in,
    dots_out,
    dots_grp,
    dots_x_out,
    dots_x,
    dots_z_out,
    dots_z,
    send_sem,
    recv_sem,
):
    sub_size = lax.axis_size("sub")
    grp_size = lax.axis_size("grp")
    z_size = sub_size // x_size
    me = lax.axis_index("sub")
    mine = lax.axis_index("grp")
    my_z, my_x = me // x_size, me % x_size
    order, columns = loads_ref.shape
    corners = coarse_ref.shape[0]
    chunk = coarse_ref.shape[1] // grp_size
    slots = pick.shape[0] // sub_size

    def sub_peer(index):
        turn = index // x_size
        reach = z_size // 2 - (turn + 1) // 2
        z = (my_z + z_size + jnp.where(turn % 2 == 1, reach, -reach)) % z_size
        x = (my_x + index + 1) % x_size
        return z * x_size + x

    def z_peer(index):
        reach = z_size // 2 - (index + 1) // 2
        z = (my_z + z_size + jnp.where(index % 2 == 1, reach, -reach)) % z_size
        return z

    def grp_peer(index):
        return (mine + 1 + index) % grp_size

    def remote(src, dst, stage, target):
        return pltpu.make_async_remote_copy(
            src_ref=src,
            dst_ref=dst,
            send_sem=send_sem.at[stage],
            recv_sem=recv_sem.at[stage],
            device_id=target,
            device_id_type=MESH,
        )

    def over_sub(body):
        lax.fori_loop(0, sub_size - 1, lambda i, c: (body(sub_peer(i)), c)[1], 0)

    def over_grp(body):
        lax.fori_loop(0, grp_size - 1, lambda i, c: (body(grp_peer(i)), c)[1], 0)

    def over_z(body):
        lax.fori_loop(0, z_size - 1, lambda i, c: (body(z_peer(i)), c)[1], 0)

    def over_x(body):
        for i in range(x_size - 1):
            body((my_x + 1 + i) % x_size)

    def wait_recv(ref, count, stage):
        view = ref.at[pl.ds(0, count)]
        remote(view, view, stage, {"sub": me, "grp": mine}).wait_recv()

    def wait_send(ref, count, stage):
        view = ref.at[pl.ds(0, count)]
        remote(view, view, stage, {"sub": me, "grp": mine}).wait_send()

    barrier = pltpu.get_barrier_semaphore()

    def greet_sub(target):
        pl.semaphore_signal(barrier, inc=1, device_id={"sub": target}, device_id_type=MESH)

    def greet_grp(target):
        pl.semaphore_signal(barrier, inc=1, device_id={"grp": target}, device_id_type=MESH)

    over_sub(greet_sub)
    over_grp(greet_grp)

    total_slots = pick.shape[0]
    row_lane = lax.broadcasted_iota(jnp.int32, (total_slots, order), 1)
    pick[...] = jnp.where(slot_col_ref[...] == row_lane, 1.0, 0.0).astype(BF16)
    row_sub = lax.broadcasted_iota(jnp.int32, (order, total_slots), 0)
    place_f = jnp.where(slot_row_ref[...] == row_sub, 1.0, 0.0)
    place[...] = place_f.astype(BF16)
    weight = 1.0 - 0.5 * jnp.sum(place_f, axis=1, keepdims=True)

    def pack(turn, field):
        packed = dot(pick[...], field).astype(BF16)
        jump_out[turn] = packed.reshape(sub_size, slots, columns)

    def send_jump(turn):
        def send(target):
            remote(
                jump_out.at[turn, target], jump_in.at[turn, me], turn, {"sub": target}
            ).start()

        over_sub(send)

    def received_jump(turn):
        wait_recv(jump_in.at[turn], sub_size - 1, turn)
        incoming = jump_in[turn].reshape(total_slots, columns)
        return dot(place[...], incoming)

    loads = loads_ref[...]
    pack(0, loads)
    empty = jnp.zeros((1, 1, slots, columns), BF16)
    for turn in range(4):
        jump_in[pl.ds(turn, 1), pl.ds(me, 1)] = empty
    map_rows = jnp.broadcast_to(map_ref[...].astype(F32), (columns, columns))
    map_out[...] = jnp.transpose(map_rows)[:CORNER_PAD]
    map_in[pl.ds(mine, 1)] = map_out[...][None]
    pad = jnp.zeros((CORNER_PAD - corners, chunk), F32)
    for g in range(grp_size):
        block = coarse_ref[:, g * chunk : (g + 1) * chunk].astype(F32)
        rows_out[g] = jnp.concatenate([block, pad], axis=0).astype(BF16)

    pl.semaphore_wait(barrier, sub_size + grp_size - 2)

    send_jump(0)

    def send_setup(target):
        remote(map_out, map_in.at[mine], 4, {"grp": target}).start()
        remote(rows_out.at[target], rows_in.at[mine], 5, {"grp": target}).start()

    over_grp(send_setup)
    rows_in[pl.ds(mine, 1)] = rows_out[pl.ds(mine, 1)]

    residual = loads.astype(F32) - received_jump(0)
    scaled = (weight * residual).astype(BF16)
    image = dot(schur_ref[...], scaled).astype(BF16)
    pack(1, image)
    send_jump(1)
    wait_recv(map_in, grp_size - 1, 4)
    wait_recv(rows_in, grp_size - 1, 5)
    corner_ids = map_in[...].reshape(grp_size * CORNER_PAD, columns)
    owned = lax.broadcasted_iota(jnp.int32, corner_ids.shape, 1) + mine * chunk
    corner_place = jnp.where(corner_ids == owned.astype(F32), 1.0, 0.0).astype(BF16)
    zfield = weight * (image.astype(F32) - received_jump(1))
    direction = zfield.astype(BF16)

    corner_part = lax.dot_general(
        couple_ref[...], direction, (((0,), (0,)), ((), ())), preferred_element_type=F32
    )
    corner_out[...] = corner_part[:CORNER_PAD].astype(BF16)

    def send_corner(target):
        remote(corner_out, corner_in.at[mine], 6, {"grp": target}).start()

    over_grp(send_corner)
    corner_in[pl.ds(mine, 1)] = corner_out[...][None]
    inner_part = jnp.sum(weight * residual * zfield, axis=0, keepdims=True)
    local_part = dot(flex_ref[...], direction)
    wait_recv(corner_in, grp_size - 1, 6)
    line_rows = corner_in[...].reshape(grp_size * CORNER_PAD, columns)
    chunk_sum = lax.dot_general(
        corner_place, line_rows, (((0,), (0,)), ((), ())), preferred_element_type=F32
    )
    piece = chunk // z_size
    zsum_out[...] = chunk_sum.reshape(z_size, piece, columns)

    def send_zsum(target):
        remote(
            zsum_out.at[target], zsum_in.at[my_z], 7, {"sub": target * x_size + my_x}
        ).start()

    over_z(send_zsum)
    zsum_in[pl.ds(my_z, 1)] = zsum_out[pl.ds(my_z, 1)]
    wait_recv(zsum_in, z_size - 1, 7)
    xsum_out[...] = jnp.sum(zsum_in[...], axis=0)

    def send_xsum(target):
        remote(xsum_out, xsum_in.at[my_x], 8, {"sub": my_z * x_size + target}).start()

    over_x(send_xsum)
    xsum_in[pl.ds(my_x, 1)] = xsum_out[...][None]
    wait_recv(xsum_in, x_size - 1, 8)
    gather_out[...] = jnp.sum(xsum_in[...], axis=0).astype(BF16).astype(F32)

    def send_gather(target):
        remote(
            gather_out, gather_in.at[my_z], 9, {"sub": target * x_size + my_x}
        ).start()

    over_z(send_gather)
    gather_in[pl.ds(my_z, 1)] = gather_out[...][None]
    wait_recv(gather_in, z_size - 1, 9)
    coarse_chunk = gather_in[...].reshape(chunk, columns).astype(BF16)
    line_matrix = rows_in[...].reshape(grp_size * CORNER_PAD, chunk)
    values = dot(line_matrix, coarse_chunk)
    val_out[...] = values.reshape(grp_size, CORNER_PAD, columns)[:, :corners]

    def send_val(target):
        remote(val_out.at[target], val_in.at[mine], 10, {"grp": target}).start()

    over_grp(send_val)
    val_in[pl.ds(mine, 1)] = val_out[pl.ds(mine, 1)]
    wait_recv(val_in, grp_size - 1, 10)
    coarse_val = jnp.sum(val_in[...], axis=0)
    val_pad = jnp.zeros((columns - corners, columns), F32)
    coarse_val = jnp.concatenate([coarse_val, val_pad], axis=0).astype(BF16)
    surface = (local_part + dot(couple_ref[...], coarse_val)).astype(BF16)
    pack(2, surface)
    send_jump(2)
    operated = surface.astype(F32) - received_jump(2)

    scaled = (weight * operated).astype(BF16)
    image = dot(schur_ref[...], scaled)
    pack(3, image.astype(BF16))
    step_part = jnp.sum(weight * zfield * operated, axis=0, keepdims=True)
    dots_pad = jnp.zeros((6, columns), F32)
    dots_out[...] = jnp.concatenate([inner_part, step_part, dots_pad], axis=0)

    def send_dots(target):
        remote(dots_out, dots_grp.at[mine], 11, {"grp": target}).start()

    over_grp(send_dots)
    send_jump(3)
    dots_grp[pl.ds(mine, 1)] = dots_out[...][None]
    wait_recv(dots_grp, grp_size - 1, 11)
    dots_x_out[...] = jnp.sum(dots_grp[...], axis=0)

    def send_dots_x(target):
        remote(dots_x_out, dots_x.at[my_x], 12, {"sub": my_z * x_size + target}).start()

    over_x(send_dots_x)
    dots_x[pl.ds(my_x, 1)] = dots_x_out[...][None]
    wait_recv(dots_x, x_size - 1, 12)
    dots_z_out[...] = jnp.sum(dots_x[...], axis=0)

    def send_dots_z(target):
        remote(
            dots_z_out, dots_z.at[my_z], 13, {"sub": target * x_size + my_x}
        ).start()

    over_z(send_dots_z)
    dots_z[pl.ds(my_z, 1)] = dots_z_out[...][None]
    wait_recv(dots_z, z_size - 1, 13)
    dots = jnp.sum(dots_z[...], axis=0)
    step = dots[0:1] / dots[1:2]
    solution_ref[...] = step * zfield
    moved = weight * (image - received_jump(3))
    precond_ref[...] = zfield - step * moved

    for turn in range(4):
        wait_send(jump_out.at[turn], sub_size - 1, turn)
    wait_send(map_in, grp_size - 1, 4)
    wait_send(rows_out, grp_size - 1, 5)
    wait_send(corner_in, grp_size - 1, 6)
    wait_send(zsum_out, z_size - 1, 7)
    wait_send(xsum_in, x_size - 1, 8)
    wait_send(gather_in, z_size - 1, 9)
    wait_send(val_out, grp_size - 1, 10)
    wait_send(dots_grp, grp_size - 1, 11)
    wait_send(dots_x, x_size - 1, 12)
    wait_send(dots_z, z_size - 1, 13)


def body(
    x_size,
    flexibility,
    dirichlet_schur,
    subdomain_loads,
    coupling,
    coarse_rows,
    neighbors,
    interface_rows,
    coarse_map,
):
    sub_size = lax.axis_size("sub")
    grp_size = lax.axis_size("grp")
    z_size = sub_size // x_size
    flex = flexibility[0, 0]
    schur = dirichlet_schur[0, 0]
    loads = subdomain_loads[0, 0]
    couple = coupling[0, 0]
    coarse = coarse_rows[0, 0]
    neighbor_ids = neighbors[0, 0]
    row_lists = interface_rows[0, 0]
    corner_ids = coarse_map[0, 0]
    order, columns = loads.shape
    corners, coarse_size = coarse.shape
    chunk = coarse_size // grp_size
    slots = row_lists.shape[1]
    match = jnp.arange(sub_size, dtype=jnp.int32)[:, None, None] == neighbor_ids[None, :, None]
    slot_rows = jnp.sum(jnp.where(match, row_lists[None] + 1, 0), axis=1) - 1
    slot_col = slot_rows.reshape(sub_size * slots, 1)
    slot_row = slot_rows.reshape(1, sub_size * slots)
    couple = jnp.pad(couple, ((0, 0), (0, columns - corners)))
    corner_ids = jnp.pad(corner_ids, (0, columns - corners), constant_values=-1)[None]
    piece = chunk // z_size
    vmem = pl.BlockSpec(memory_space=pltpu.VMEM)
    return tuple(
        out[None, None]
        for out in pl.pallas_call(
            functools.partial(kernel, x_size),
            name="dual_iteration",
            out_shape=(jax.ShapeDtypeStruct((order, columns), F32),) * 2,
            in_specs=[vmem] * 8,
            out_specs=(vmem, vmem),
            scratch_shapes=[
                pltpu.VMEM((sub_size * slots, order), BF16),
                pltpu.VMEM((order, sub_size * slots), BF16),
                pltpu.VMEM((4, sub_size, slots, columns), BF16),
                pltpu.VMEM((4, sub_size, slots, columns), BF16),
                pltpu.VMEM((CORNER_PAD, columns), F32),
                pltpu.VMEM((grp_size, CORNER_PAD, columns), F32),
                pltpu.VMEM((grp_size, CORNER_PAD, chunk), BF16),
                pltpu.VMEM((grp_size, CORNER_PAD, chunk), BF16),
                pltpu.VMEM((CORNER_PAD, columns), BF16),
                pltpu.VMEM((grp_size, CORNER_PAD, columns), BF16),
                pltpu.VMEM((z_size, piece, columns), F32),
                pltpu.VMEM((z_size, piece, columns), F32),
                pltpu.VMEM((piece, columns), F32),
                pltpu.VMEM((x_size, piece, columns), F32),
                pltpu.VMEM((piece, columns), F32),
                pltpu.VMEM((z_size, piece, columns), F32),
                pltpu.VMEM((grp_size, corners, columns), F32),
                pltpu.VMEM((grp_size, corners, columns), F32),
                pltpu.VMEM((8, columns), F32),
                pltpu.VMEM((grp_size, 8, columns), F32),
                pltpu.VMEM((8, columns), F32),
                pltpu.VMEM((x_size, 8, columns), F32),
                pltpu.VMEM((8, columns), F32),
                pltpu.VMEM((z_size, 8, columns), F32),
                pltpu.SemaphoreType.DMA((14,)),
                pltpu.SemaphoreType.DMA((14,)),
            ],
            compiler_params=pltpu.CompilerParams(
                collective_id=0,
                has_side_effects=True,
                vmem_limit_bytes=48 << 20,
            ),
        )(flex, schur, loads, couple, coarse, slot_col, slot_row, corner_ids)
    )


def solution(mesh, x_size=4):
    placed = (
        P("sub", "grp", None, None),
        P("sub", "grp", None, None),
        P("sub", "grp", None, None),
        P("sub", "grp", None, None),
        P("sub", "grp", None, None),
        P("sub", "grp", None),
        P("sub", "grp", None, None),
        P("sub", "grp", None),
    )
    return jax.shard_map(
        functools.partial(body, x_size),
        mesh=mesh,
        in_specs=placed,
        out_specs=(P("sub", "grp", None, None), P("sub", "grp", None, None)),
        check_vma=False,
    )
```

time: 1130 us -> 129 us (0.11)
  waiting for transfers between devices: 742 us -> 0 us
  blocking collectives: 303 us -> 0 us
  Pallas kernels: 0 us -> 123 us
  starting transfers between devices: 37.4 us -> 0 us
  local copies, waits for them, and re-layouts: 26.7 us -> 4.52 us
  between operations: 14.4 us -> 0.76 us
    reduce_scatter x1 -> x0, waiting for transfers between devices: 688 us -> none  [body(): lax.psum_scatter(dense_sum, 'sub', scatter_dimension=0, tiled=True)]
    psum x2 -> x0, blocking collectives: 202 us -> none  [the longest x1 148 us: column_dot(): lax.psum(jnp.sum(weight * first_field * second_field, axis=0), ('sub', 'g...]
    pallas_call x0 -> x1, Pallas kernels: none -> 123 us  [body(): pl.pallas_call(functools.partial(kernel, x_size), name='dual_iteration',...]
    all_gather x1 -> x0, blocking collectives: 72.5 us -> none  [body(): lax.all_gather(panel_half, 'sub', axis=0, tiled=True)]
    all_to_all x3 -> x0, waiting for transfers between devices: 53.5 us -> none  [jump_field(): lax.all_to_all(outgoing, 'sub', split_axis=0, concat_axis=0, tiled=True)]
    all_to_all x3 -> x0, starting transfers between devices: 37.4 us -> none  [jump_field(): lax.all_to_all(outgoing, 'sub', split_axis=0, concat_axis=0, tiled=True)]
    all_to_all x1 -> x0, blocking collectives: 28.5 us -> none  [jump_field(): lax.all_to_all(outgoing, 'sub', split_axis=0, concat_axis=0, tiled=True)]
    scatter x10 -> x0, local copies, waits for them, and re-layouts: 11.7 us -> none  [the longest x8 7.07 us: jump_field(): placed = jnp.zeros((order_size, column_count), jnp.float32).at[flat_rows]...]
  transfers between devices with their start and end apart: 4 -> 0, of which waited for: 4 -> 0; matrix products, arithmetic and copies ran while one was open for 0% -> 0% of each run, Pallas kernels for 0% -> 0%
where the time goes in v1:
time: 129 us; the launch traced here: 128 us
  Pallas kernels  123 us (95%)
  local copies, waits for them, and re-layouts  4.52 us (4%)
    pallas_call x1, Pallas kernels, body(): pl.pallas_call(functools.partial(kernel, x_size), name='dual_iteration',...  123 us
    unnamed x17, local copies, waits for them, and re-layouts  3.94 us

profile of v1, /device:TPU:1, one launch (start us, length us, event | category | flops | bytes accessed | tf_op | source)
XLA Modules:
  0.0 128.4 jit_solution(10447483509739326059)
XLA Ops:
  0.6 0.0 copy-start.4
  0.6 0.0 copy-start.6
  0.7 0.0 copy-start.5
  0.7 0.0 copy-start.3
  0.7 0.6 copy-done.6
  1.3 0.0 copy-done.5
  1.3 0.1 iota_compare_fusion
  1.4 0.0 copy-done.4
  1.4 0.1 copy.16
  1.5 0.1 select_reduce_fusion
  1.6 0.0 copy-start
  1.6 0.0 copy-start.1
  1.7 0.1 copy.17
  1.7 0.1 sub.10.slot_row_ref
  1.8 1.0 copy.15
  2.8 0.3 sub.11.slot_col_ref
  3.1 0.0 copy-done.3
  3.1 0.0 copy-done
  3.1 0.0 copy-done.1
  3.2 0.0 copy-start.2
  3.2 0.9 copy-done.2
  4.1 122.9 %dual_iteration.1 = (f32[512,128]{1,0:T(8,128)S(1)}, f32[512,128]{1,0:T(8,128)S(1)}) custom-call(bf16[512,512]{1,0:T(8,128)(2,1)S(1)} %bitcast.13, bf16[512,512]{1,0:T(8,128)(2,1)S(1)} %bitcast.14, bf16[512,128]{1,0:T(8,128)(2,1)S(1)} %bitcast.17, bf16[512,128]{1,0:T(8,128)(2,1)S(1)} %pad.8.couple_ref, bf16[24,2048]{1,0:T(8,128)(2,1)S(1)} %bitcast.18, ...), custom_call_target="tpu_custom_call" | custom-call | tf_op jit(solution)/shard_map/dual_iteration/pallas_call | solution.py:342
  127.0 0.7 copy.22
  127.7 0.7 copy.23
  (4 shorter events, 0.0 us)
Async XLA Ops:
  0.6 0.8 copy-start.4
  0.6 0.7 copy-start.6
  0.7 0.7 copy-start.5
  0.7 2.5 %copy-start.3 = (bf16[1,1,24,2048]{3,2,1,0:T(8,128)(2,1)S(1)}, bf16[1,1,24,2048]{3,2,1,0:T(8,128)(2,1)}, u32[]{:S(2)}) copy-start(bf16[1,1,24,2048]{3,2,1,0:T(8,128)(2,1)} %param.12) | copy-start | bytes 294916
  1.6 1.5 %copy-start = (bf16[1,1,512,512]{3,2,1,0:T(8,128)(2,1)S(1)}, bf16[1,1,512,512]{3,2,1,0:T(8,128)(2,1)}, u32[]{:S(2)}) copy-start(bf16[1,1,512,512]{3,2,1,0:T(8,128)(2,1)} %param.8) | copy-start | bytes 1572868
  1.6 1.5 %copy-start.1 = (bf16[1,1,512,512]{3,2,1,0:T(8,128)(2,1)S(1)}, bf16[1,1,512,512]{3,2,1,0:T(8,128)(2,1)}, u32[]{:S(2)}) copy-start(bf16[1,1,512,512]{3,2,1,0:T(8,128)(2,1)} %param.9) | copy-start | bytes 1572868
  3.2 0.9 copy-start.2

commit v2 on v1

v2 whole, which is shorter than its diff:
```python
import functools

import jax
import jax.numpy as jnp
from jax import lax
from jax.experimental import pallas as pl
from jax.experimental.pallas import tpu as pltpu
from jax.sharding import PartitionSpec as P

F32 = jnp.float32
BF16 = jnp.bfloat16
MESH = pl.DeviceIdType.MESH
CORNER_PAD = 32


def dot(a, b):
    return jnp.dot(a, b, preferred_element_type=F32)


def kernel(
    x_size,
    flex_ref,
    schur_ref,
    loads_hbm,
    couple_t_ref,
    coarse_ref,
    slot_col_ref,
    slot_row_ref,
    map_ref,
    base_ref,
    moved_ref,
    step_ref,
    loads_ref,
    pick,
    place,
    couple,
    jump_out,
    jump_in,
    map_out,
    map_in,
    rows_out,
    rows_in,
    corner_out,
    corner_in,
    zsum_out,
    zsum_in,
    xsum_out,
    xsum_in,
    gather_out,
    gather_in,
    val_out,
    val_in,
    dots_out,
    dots_grp,
    dots_x_out,
    dots_x,
    dots_z_out,
    dots_z,
    load_sem,
    send_sem,
    recv_sem,
):
    sub_size = lax.axis_size("sub")
    grp_size = lax.axis_size("grp")
    z_size = sub_size // x_size
    me = lax.axis_index("sub")
    mine = lax.axis_index("grp")
    my_z, my_x = me // x_size, me % x_size
    order, columns = loads_ref.shape
    corners = coarse_ref.shape[0]
    chunk = coarse_ref.shape[1] // grp_size
    total_slots = pick.shape[0]
    half_slots = total_slots // 2
    half_corners = CORNER_PAD // 2
    width = columns // 2
    halves = (0, 1)

    def z_peer(index):
        reach = z_size // 2 - (index + 1) // 2
        return (my_z + z_size + jnp.where(index % 2 == 1, reach, -reach)) % z_size

    def sub_peer(index):
        return z_peer(index // x_size) * x_size + (my_x + index + 1) % x_size

    def grp_peer(index):
        return (mine + 1 + index) % grp_size

    def remote(src, dst, stage, target):
        return pltpu.make_async_remote_copy(
            src_ref=src,
            dst_ref=dst,
            send_sem=send_sem.at[stage],
            recv_sem=recv_sem.at[stage],
            device_id=target,
            device_id_type=MESH,
        )

    def over_sub(body):
        lax.fori_loop(0, sub_size - 1, lambda i, c: (body(sub_peer(i)), c)[1], 0)

    def over_grp(body):
        lax.fori_loop(0, grp_size - 1, lambda i, c: (body(grp_peer(i)), c)[1], 0)

    def over_z(body):
        lax.fori_loop(0, z_size - 1, lambda i, c: (body(z_peer(i)), c)[1], 0)

    def over_x(body):
        for i in range(x_size - 1):
            body((my_x + 1 + i) % x_size)

    def on_z(target):
        return {"sub": target * x_size + my_x}

    def on_x(target):
        return {"sub": my_z * x_size + target}

    def wait_recv(ref, count, stage):
        view = ref.at[pl.ds(0, count)]
        remote(view, view, stage, {"sub": me, "grp": mine}).wait_recv()

    def wait_send(ref, count, stage):
        view = ref.at[pl.ds(0, count)]
        remote(view, view, stage, {"sub": me, "grp": mine}).wait_send()

    def fold(field):
        rows = field.shape[0] // 2
        return jnp.concatenate([field[:rows], field[rows:]], axis=1)

    def unfold(block):
        return jnp.concatenate([block[:, :width], block[:, width:]], axis=0)

    load = pltpu.make_async_copy(loads_hbm, loads_ref, load_sem)
    load.start()

    barrier = pltpu.get_barrier_semaphore()

    def greet_sub(target):
        pl.semaphore_signal(barrier, inc=1, device_id={"sub": target}, device_id_type=MESH)

    def greet_grp(target):
        pl.semaphore_signal(barrier, inc=1, device_id={"grp": target}, device_id_type=MESH)

    over_sub(greet_sub)
    over_grp(greet_grp)

    row_lane = lax.broadcasted_iota(jnp.int32, (total_slots, order), 1)
    pick[...] = jnp.where(slot_col_ref[...] == row_lane, 1.0, 0.0).astype(BF16)
    row_sub = lax.broadcasted_iota(jnp.int32, (order, total_slots), 0)
    place_f = jnp.where(slot_row_ref[...] == row_sub, 1.0, 0.0)
    place[...] = place_f.astype(BF16)
    weight = 1.0 - 0.5 * jnp.sum(place_f, axis=1, keepdims=True)

    def jump_stage(turn, h):
        return turn * 2 + h

    def pack(turn, h, field):
        packed = fold(dot(pick[...], field))
        jump_out[turn, h] = packed.reshape(jump_out.shape[2:]).astype(BF16)

    def send_jump(turn, h):
        def send(target):
            remote(
                jump_out.at[turn, h, target],
                jump_in.at[turn, h, me],
                jump_stage(turn, h),
                {"sub": target},
            ).start()

        over_sub(send)

    def received_jump(turn, h):
        wait_recv(jump_in.at[turn, h], sub_size - 1, jump_stage(turn, h))
        incoming = jump_in[turn, h].astype(F32).reshape(half_slots, columns).astype(BF16)
        first = dot(place[:, :half_slots], incoming)
        second = dot(place[:, half_slots:], incoming)
        return first[:, :width] + second[:, width:]

    load.wait()
    loads = [loads_ref[:, h * width : (h + 1) * width] for h in halves]
    for h in halves:
        pack(0, h, loads[h])
    empty = jnp.zeros((1, 1, 1) + jump_in.shape[3:], BF16)
    for turn in range(4):
        for h in halves:
            jump_in[pl.ds(turn, 1), pl.ds(h, 1), pl.ds(me, 1)] = empty
    map_rows = jnp.broadcast_to(map_ref[...].astype(F32), (columns, columns))
    map_out[...] = jnp.transpose(map_rows)[:CORNER_PAD]
    map_in[pl.ds(mine, 1)] = map_out[...][None]
    pad = jnp.zeros((CORNER_PAD - corners, chunk), F32)
    for g in range(grp_size):
        block = coarse_ref[:, g * chunk : (g + 1) * chunk].astype(F32)
        rows_out[g] = jnp.concatenate([block, pad], axis=0).astype(BF16)

    pl.semaphore_wait(barrier, sub_size + grp_size - 2)

    for h in halves:
        send_jump(0, h)

    def send_setup(target):
        remote(map_out, map_in.at[mine], 8, {"grp": target}).start()
        remote(rows_out.at[target], rows_in.at[mine], 9, {"grp": target}).start()

    over_grp(send_setup)
    rows_in[pl.ds(mine, 1)] = rows_out[pl.ds(mine, 1)]
    couple_pad = jnp.zeros((columns - corners, order), F32)
    couple_full = jnp.concatenate([couple_t_ref[...].astype(F32), couple_pad], axis=0)
    couple[...] = jnp.transpose(couple_full).astype(BF16)

    residual, image = [None, None], [None, None]
    for h in halves:
        residual[h] = loads[h].astype(F32) - received_jump(0, h)
        scaled = (weight * residual[h]).astype(BF16)
        image[h] = dot(schur_ref[...], scaled).astype(BF16)
        pack(1, h, image[h])
        send_jump(1, h)
    wait_recv(map_in, grp_size - 1, 8)
    wait_recv(rows_in, grp_size - 1, 9)
    corner_ids = map_in[...].reshape(grp_size * CORNER_PAD, columns)
    owned = lax.broadcasted_iota(jnp.int32, corner_ids.shape, 1) + mine * chunk
    corner_place = jnp.where(corner_ids == owned.astype(F32), 1.0, 0.0).astype(BF16)

    zfield, local_part, inner_part = [None, None], [None, None], [None, None]
    corner_pad = jnp.zeros((CORNER_PAD - corners, width), F32)
    for h in halves:
        zfield[h] = weight * (image[h].astype(F32) - received_jump(1, h))
        direction = zfield[h].astype(BF16)
        corner_part = jnp.concatenate([dot(couple_t_ref[...], direction), corner_pad], axis=0)
        corner_out[h] = fold(corner_part).astype(BF16)

        def send_corner(target, h=h):
            remote(corner_out.at[h], corner_in.at[h, mine], 10 + h, {"grp": target}).start()

        over_grp(send_corner)
        corner_in[h, pl.ds(mine, 1)] = corner_out[h][None]
        inner_part[h] = jnp.sum(weight * residual[h] * zfield[h], axis=0, keepdims=True)
        local_part[h] = dot(flex_ref[...], direction)

    for h in halves:
        base_ref[:, h * width : (h + 1) * width] = zfield[h]
    for h in halves:
        wait_recv(corner_in.at[h], grp_size - 1, 10 + h)
        line_rows = jnp.concatenate(
            [corner_in[h, :, :, :width], corner_in[h, :, :, width:]], axis=1
        ).reshape(grp_size * CORNER_PAD, width)
        chunk_sum = lax.dot_general(
            corner_place, line_rows, (((0,), (0,)), ((), ())), preferred_element_type=F32
        )
        zsum_out[h] = fold(chunk_sum).reshape(zsum_out.shape[1:])

        def send_zsum(target, h=h):
            remote(
                zsum_out.at[h, target], zsum_in.at[h, my_z], 12 + h, on_z(target)
            ).start()

        over_z(send_zsum)
        zsum_in[h, pl.ds(my_z, 1)] = zsum_out[h, pl.ds(my_z, 1)]
    for h in halves:
        wait_recv(zsum_in.at[h], z_size - 1, 12 + h)
        xsum_out[h] = jnp.sum(zsum_in[h], axis=0)

        def send_xsum(target, h=h):
            remote(xsum_out.at[h], xsum_in.at[h, my_x], 14 + h, on_x(target)).start()

        over_x(send_xsum)
        xsum_in[h, pl.ds(my_x, 1)] = xsum_out[h][None]
    for h in halves:
        wait_recv(xsum_in.at[h], x_size - 1, 14 + h)
        gather_out[h] = jnp.sum(xsum_in[h], axis=0).astype(BF16).astype(F32)

        def send_gather(target, h=h):
            remote(gather_out.at[h], gather_in.at[h, my_z], 16 + h, on_z(target)).start()

        over_z(send_gather)
        gather_in[h, pl.ds(my_z, 1)] = gather_out[h][None]
    line_matrix = rows_in[...].reshape(grp_size * CORNER_PAD, chunk)
    for h in halves:
        wait_recv(gather_in.at[h], z_size - 1, 16 + h)
        coarse_chunk = unfold(gather_in[h].reshape(chunk // 2, columns)).astype(BF16)
        values = dot(line_matrix, coarse_chunk).reshape(grp_size, CORNER_PAD, width)
        val_out[h] = jnp.concatenate(
            [values[:, :half_corners], values[:, half_corners:]], axis=2
        ).astype(BF16)

        def send_val(target, h=h):
            remote(
                val_out.at[h, target], val_in.at[h, mine], 18 + h, {"grp": target}
            ).start()

        over_grp(send_val)
        val_in[h, pl.ds(mine, 1)] = val_out[h, pl.ds(mine, 1)]
    surface, step_part = [None, None], [None, None]
    for h in halves:
        wait_recv(val_in.at[h], grp_size - 1, 18 + h)
        coarse_val = unfold(jnp.sum(val_in[h].astype(F32), axis=0)).astype(BF16)
        correction = dot(couple[:, :CORNER_PAD], coarse_val)
        surface[h] = (local_part[h] + correction).astype(BF16)
        pack(2, h, surface[h])
        send_jump(2, h)
        step_part[h] = jnp.sum(zfield[h] * surface[h].astype(F32), axis=0, keepdims=True)

    dots_pad = jnp.zeros((6, columns), F32)
    dots_out[...] = jnp.concatenate(
        [
            jnp.concatenate(inner_part, axis=1),
            jnp.concatenate(step_part, axis=1),
            dots_pad,
        ],
        axis=0,
    )

    def send_dots(target):
        remote(dots_out, dots_grp.at[mine], 20, {"grp": target}).start()

    over_grp(send_dots)
    dots_grp[pl.ds(mine, 1)] = dots_out[...][None]

    image = [None, None]
    for h in halves:
        operated = surface[h].astype(F32) - received_jump(2, h)
        scaled = (weight * operated).astype(BF16)
        image[h] = dot(schur_ref[...], scaled)
        pack(3, h, image[h].astype(BF16))
        send_jump(3, h)
        if h == 0:
            wait_recv(dots_grp, grp_size - 1, 20)
            dots_x_out[...] = jnp.sum(dots_grp[...], axis=0)

            def send_dots_x(target):
                remote(dots_x_out, dots_x.at[my_x], 21, on_x(target)).start()

            over_x(send_dots_x)
            dots_x[pl.ds(my_x, 1)] = dots_x_out[...][None]
    wait_recv(dots_x, x_size - 1, 21)
    dots_z_out[...] = jnp.sum(dots_x[...], axis=0)

    def send_dots_z(target):
        remote(dots_z_out, dots_z.at[my_z], 22, on_z(target)).start()

    over_z(send_dots_z)
    dots_z[pl.ds(my_z, 1)] = dots_z_out[...][None]

    for turn in range(3):
        for h in halves:
            wait_send(jump_out.at[turn, h], sub_size - 1, jump_stage(turn, h))
    wait_send(map_in, grp_size - 1, 8)
    wait_send(rows_out, grp_size - 1, 9)
    for h in halves:
        wait_send(corner_in.at[h], grp_size - 1, 10 + h)
        wait_send(zsum_out.at[h], z_size - 1, 12 + h)
        wait_send(xsum_in.at[h], x_size - 1, 14 + h)
        wait_send(gather_in.at[h], z_size - 1, 16 + h)
        wait_send(val_out.at[h], grp_size - 1, 18 + h)
    wait_send(dots_grp, grp_size - 1, 20)
    wait_send(dots_x, x_size - 1, 21)

    moved_ref[:, :width] = weight * (image[0] - received_jump(3, 0))
    wait_recv(dots_z, z_size - 1, 22)
    dots = jnp.sum(dots_z[...], axis=0)
    step_ref[...] = dots[0:1] / dots[1:2]
    moved_ref[:, width:] = weight * (image[1] - received_jump(3, 1))
    for h in halves:
        wait_send(jump_out.at[3, h], sub_size - 1, jump_stage(3, h))
    wait_send(dots_z, z_size - 1, 22)


def body(
    x_size,
    flexibility,
    dirichlet_schur,
    subdomain_loads,
    coupling,
    coarse_rows,
    neighbors,
    interface_rows,
    coarse_map,
):
    sub_size = lax.axis_size("sub")
    grp_size = lax.axis_size("grp")
    z_size = sub_size // x_size
    flex = flexibility[0, 0]
    schur = dirichlet_schur[0, 0]
    loads = subdomain_loads[0, 0]
    couple_t = coupling[0, 0].T
    coarse = coarse_rows[0, 0]
    neighbor_ids = neighbors[0, 0]
    row_lists = interface_rows[0, 0]
    corner_ids = coarse_map[0, 0]
    order, columns = loads.shape
    corners, coarse_size = coarse.shape
    chunk = coarse_size // grp_size
    slots = row_lists.shape[1]
    total_slots = sub_size * slots
    match = jnp.arange(sub_size, dtype=jnp.int32)[:, None, None] == neighbor_ids[None, :, None]
    slot_rows = jnp.sum(jnp.where(match, row_lists[None] + 1, 0), axis=1) - 1
    slot_rows = slot_rows.reshape(sub_size, 2, slots // 2).transpose(1, 0, 2)
    slot_col = slot_rows.reshape(total_slots, 1)
    slot_row = slot_rows.reshape(1, total_slots)
    corner_ids = jnp.pad(corner_ids, (0, columns - corners), constant_values=-1)[None]
    piece = chunk // 2 // z_size
    fold = CORNER_PAD // 2
    vmem = pl.BlockSpec(memory_space=pltpu.VMEM)
    hbm = pl.BlockSpec(memory_space=pltpu.HBM)
    base, moved, step = pl.pallas_call(
        functools.partial(kernel, x_size),
        name="dual_iteration",
        out_shape=(
            jax.ShapeDtypeStruct((order, columns), F32),
            jax.ShapeDtypeStruct((order, columns), F32),
            jax.ShapeDtypeStruct((1, columns), F32),
        ),
        in_specs=[vmem, vmem, hbm, vmem, vmem, vmem, vmem, vmem],
        out_specs=(vmem, vmem, vmem),
        scratch_shapes=[
            pltpu.VMEM((order, columns), BF16),
            pltpu.VMEM((total_slots, order), BF16),
            pltpu.VMEM((order, total_slots), BF16),
            pltpu.VMEM((order, columns), BF16),
            pltpu.VMEM((4, 2, sub_size, slots // 2, columns), BF16),
            pltpu.VMEM((4, 2, sub_size, slots // 2, columns), BF16),
            pltpu.VMEM((CORNER_PAD, columns), F32),
            pltpu.VMEM((grp_size, CORNER_PAD, columns), F32),
            pltpu.VMEM((grp_size, CORNER_PAD, chunk), BF16),
            pltpu.VMEM((grp_size, CORNER_PAD, chunk), BF16),
            pltpu.VMEM((2, fold, columns), BF16),
            pltpu.VMEM((2, grp_size, fold, columns), BF16),
            pltpu.VMEM((2, z_size, piece, columns), F32),
            pltpu.VMEM((2, z_size, piece, columns), F32),
            pltpu.VMEM((2, piece, columns), F32),
            pltpu.VMEM((2, x_size, piece, columns), F32),
            pltpu.VMEM((2, piece, columns), F32),
            pltpu.VMEM((2, z_size, piece, columns), F32),
            pltpu.VMEM((2, grp_size, fold, columns), BF16),
            pltpu.VMEM((2, grp_size, fold, columns), BF16),
            pltpu.VMEM((8, columns), F32),
            pltpu.VMEM((grp_size, 8, columns), F32),
            pltpu.VMEM((8, columns), F32),
            pltpu.VMEM((x_size, 8, columns), F32),
            pltpu.VMEM((8, columns), F32),
            pltpu.VMEM((z_size, 8, columns), F32),
            pltpu.SemaphoreType.DMA,
            pltpu.SemaphoreType.DMA((23,)),
            pltpu.SemaphoreType.DMA((23,)),
        ],
        compiler_params=pltpu.CompilerParams(
            collective_id=0,
            has_side_effects=True,
            vmem_limit_bytes=48 << 20,
        ),
    )(flex, schur, loads, couple_t, coarse, slot_col, slot_row, corner_ids)
    return ((step * base)[None, None], (base - step * moved)[None, None])


def solution(mesh, x_size=4):
    placed = (
        P("sub", "grp", None, None),
        P("sub", "grp", None, None),
        P("sub", "grp", None, None),
        P("sub", "grp", None, None),
        P("sub", "grp", None, None),
        P("sub", "grp", None),
        P("sub", "grp", None, None),
        P("sub", "grp", None),
    )
    return jax.shard_map(
        functools.partial(body, x_size),
        mesh=mesh,
        in_specs=placed,
        out_specs=(P("sub", "grp", None, None), P("sub", "grp", None, None)),
        check_vma=False,
    )
```

time: 129 us -> 115 us (0.89)
  Pallas kernels: 123 us -> 109 us
  local copies, waits for them, and re-layouts: 4.52 us -> 2.97 us
  other arithmetic: 0.21 us -> 1.69 us
    pallas_call x1, Pallas kernels: 123 us -> 109 us  [body(): pl.pallas_call(functools.partial(kernel, x_size), name='dual_iteration',...]
    unnamed x17 -> x12, local copies, waits for them, and re-layouts: 3.94 us -> 1.79 us
where the time goes in v2:
time: 115 us
  Pallas kernels  109 us (95%)
  local copies, waits for them, and re-layouts  2.97 us (3%)
  other arithmetic  1.69 us (1%)
    pallas_call x1, Pallas kernels, body(): pl.pallas_call(functools.partial(kernel, x_size), name='dual_iteration',...  109 us

profile of v2, /device:TPU:1, one launch (start us, length us, event | category | flops | bytes accessed | tf_op | source)
XLA Modules:
  0.0 114.7 jit_solution(11926613518999603220)
XLA Ops:
  0.6 0.0 copy-start.5
  0.6 0.0 copy-start
  0.6 0.7 pad_bitcast_fusion.map_ref
  1.4 0.7 iota_compare_fusion
  2.1 0.0 copy-done.5
  2.1 0.1 copy.15
  2.2 0.1 select_reduce_fusion
  2.3 0.1 copy.16
  2.4 0.1 reshape.49.slot_row_ref
  2.5 0.0 copy-start.2
  2.5 0.0 copy-start.3
  2.6 0.0 copy-start.4
  2.6 0.2 reshape.50.slot_col_ref
  2.8 0.0 copy-done
  2.8 0.7 copy-done.2
  3.4 0.1 copy-done.3
  3.5 0.0 copy-done.4
  3.5 0.0 copy-start.1
  3.5 1.0 copy-done.1
  4.5 109.3 %dual_iteration.1 = (f32[512,128]{1,0:T(8,128)S(1)}, f32[512,128]{1,0:T(8,128)S(1)}, f32[1,128]{1,0:T(1,128)S(1)}) custom-call(bf16[512,512]{1,0:T(8,128)(2,1)S(1)} %bitcast.22, bf16[512,512]{1,0:T(8,128)(2,1)S(1)} %bitcast.23, bf16[512,128]{1,0:T(8,128)(2,1)S(1)} %bitcast.24, bf16[24,512]{1,0:T(8,128)(2,1)S(1)} %bitcast.26, bf16[24,2048]{1,0:T(8,128)(2,1)S(1)} %bitcast.25, ...), custom_call_target="tpu_custom_call" | custom-call | tf_op jit(solution)/shard_map/dual_iteration/pallas_call | solution.py:403
  113.9 0.8 subtract_bitcast_fusion
  (2 shorter events, 0.0 us)
Async XLA Ops:
  0.6 1.5 %copy-start.5 = (s32[1,1,28,16]{2,3,1,0:T(8,128)S(1)}, s32[1,1,28,16]{2,3,1,0:T(8,128)}, u32[]{:S(2)}) copy-start(s32[1,1,28,16]{2,3,1,0:T(8,128)} %param.14) | copy-start | bytes 5380
  0.6 2.1 %copy-start = (bf16[1,1,512,512]{3,2,1,0:T(8,128)(2,1)S(1)}, bf16[1,1,512,512]{3,2,1,0:T(8,128)(2,1)}, u32[]{:S(2)}) copy-start(bf16[1,1,512,512]{3,2,1,0:T(8,128)(2,1)} %param.8) | copy-start | bytes 1572868
  2.5 0.9 copy-start.2
  2.5 1.0 copy-start.3
  2.6 0.9 copy-start.4
  3.5 1.0 copy-start.1

commit v3 on v2

--- a/solution.py
+++ b/solution.py
@@ -13,24 +13,35 @@
 CORNER_PAD = 32
 
 
+def log2(size):
+    return size.bit_length() - 1
+
+
 def dot(a, b):
     return jnp.dot(a, b, preferred_element_type=F32)
 
 
 def kernel(
     x_size,
-    flex_ref,
-    schur_ref,
+    flex_hbm,
+    schur_hbm,
     loads_hbm,
-    couple_t_ref,
-    coarse_ref,
-    slot_col_ref,
-    slot_row_ref,
-    map_ref,
+    couple_t_hbm,
+    coarse_hbm,
+    neighbors_hbm,
+    row_lists_hbm,
+    map_hbm,
     base_ref,
     moved_ref,
     step_ref,
+    flex_ref,
+    schur_ref,
     loads_ref,
+    couple_t_ref,
+    coarse_ref,
+    neighbors_ref,
+    row_lists_ref,
+    map_ref,
     pick,
     place,
     couple,
@@ -69,6 +80,7 @@
     order, columns = loads_ref.shape
     corners = coarse_ref.shape[0]
     chunk = coarse_ref.shape[1] // grp_size
+    slots = row_lists_ref.shape[0]
     total_slots = pick.shape[0]
     half_slots = total_slots // 2
     half_corners = CORNER_PAD // 2
@@ -78,9 +90,6 @@
     def z_peer(index):
         reach = z_size // 2 - (index + 1) // 2
         return (my_z + z_size + jnp.where(index % 2 == 1, reach, -reach)) % z_size
-
-    def sub_peer(index):
-        return z_peer(index // x_size) * x_size + (my_x + index + 1) % x_size
 
     def grp_peer(index):
         return (mine + 1 + index) % grp_size
@@ -95,8 +104,18 @@
             device_id_type=MESH,
         )
 
+    x_order = [(my_x + 1 + i) % x_size for i in range(x_size)]
+
     def over_sub(body):
-        lax.fori_loop(0, sub_size - 1, lambda i, c: (body(sub_peer(i)), c)[1], 0)
+        def turn(index, carry):
+            start = z_peer(index) * x_size
+            for x in x_order:
+                body(start + x)
+            return carry
+
+        lax.fori_loop(0, z_size - 1, turn, 0)
+        for x in x_order[:-1]:
+            body(my_z * x_size + x)
 
     def over_grp(body):
         lax.fori_loop(0, grp_size - 1, lambda i, c: (body(grp_peer(i)), c)[1], 0)
@@ -105,8 +124,8 @@
         lax.fori_loop(0, z_size - 1, lambda i, c: (body(z_peer(i)), c)[1], 0)
 
     def over_x(body):
-        for i in range(x_size - 1):
-            body((my_x + 1 + i) % x_size)
+        for x in x_order[:-1]:
+            body(x)
 
     def on_z(target):
         return {"sub": target * x_size + my_x}
@@ -129,8 +148,23 @@
     def unfold(block):
         return jnp.concatenate([block[:, :width], block[:, width:]], axis=0)
 
-    load = pltpu.make_async_copy(loads_hbm, loads_ref, load_sem)
-    load.start()
+    loading = [
+        pltpu.make_async_copy(src, dst, load_sem.at[i])
+        for i, (src, dst) in enumerate(
+            (
+                (neighbors_hbm, neighbors_ref),
+                (row_lists_hbm, row_lists_ref),
+                (loads_hbm, loads_ref),
+                (map_hbm, map_ref),
+                (coarse_hbm, coarse_ref),
+                (couple_t_hbm, couple_t_ref),
+                (schur_hbm, schur_ref),
+                (flex_hbm, flex_ref),
+            )
+        )
+    ]
+    for copy in loading:
+        copy.start()
 
     barrier = pltpu.get_barrier_semaphore()
 
@@ -143,13 +177,31 @@
     over_sub(greet_sub)
     over_grp(greet_grp)
 
+    for copy in loading[:2]:
+        copy.wait()
+    half = slots // 2
+    nt = (((1,), (1,)), ((), ()))
+    listed = lax.broadcasted_iota(jnp.int32, (sub_size, neighbors_ref.shape[1]), 0)
+    match = jnp.where(listed == neighbors_ref[...], 1.0, 0.0).astype(BF16)
+    shifted = row_lists_ref[...] + 1
+    digits = (jnp.right_shift(shifted, 5), jnp.bitwise_and(shifted, 31))
+    digits = [d.astype(F32).astype(BF16) for d in digits]
+
+    def split(slot):
+        low = jnp.bitwise_and(slot, half - 1)
+        line = jnp.bitwise_and(jnp.right_shift(slot, log2(half)), sub_size - 1)
+        return line, low + half * jnp.right_shift(slot, log2(half * sub_size))
+
+    line, _ = split(lax.broadcasted_iota(jnp.int32, (total_slots, sub_size), 0))
+    _, low = split(lax.broadcasted_iota(jnp.int32, (total_slots, slots), 0))
+    spread = lax.broadcasted_iota(jnp.int32, line.shape, 1) == line
+    spread = jnp.where(spread, 1.0, 0.0).astype(BF16)
+    by_line = [lax.dot_general(match, d, nt, preferred_element_type=F32) for d in digits]
+    column = 32.0 * dot(spread, by_line[0].astype(BF16)) + dot(spread, by_line[1].astype(BF16))
+    chosen = lax.broadcasted_iota(jnp.int32, column.shape, 1) == low
+    column = jnp.sum(jnp.where(chosen, column, 0.0), axis=1, keepdims=True).astype(jnp.int32) - 1
     row_lane = lax.broadcasted_iota(jnp.int32, (total_slots, order), 1)
-    pick[...] = jnp.where(slot_col_ref[...] == row_lane, 1.0, 0.0).astype(BF16)
-    row_sub = lax.broadcasted_iota(jnp.int32, (order, total_slots), 0)
-    place_f = jnp.where(slot_row_ref[...] == row_sub, 1.0, 0.0)
-    place[...] = place_f.astype(BF16)
-    weight = 1.0 - 0.5 * jnp.sum(place_f, axis=1, keepdims=True)
-
+    pick[...] = jnp.where(column == row_lane, 1.0, 0.0).astype(BF16)
     def jump_stage(turn, h):
         return turn * 2 + h
 
@@ -175,15 +227,23 @@
         second = dot(place[:, half_slots:], incoming)
         return first[:, :width] + second[:, width:]
 
-    load.wait()
+    loading[2].wait()
     loads = [loads_ref[:, h * width : (h + 1) * width] for h in halves]
-    for h in halves:
-        pack(0, h, loads[h])
+    pack(0, 0, loads[0])
+    pl.semaphore_wait(barrier, sub_size + grp_size - 2)
+
+    send_jump(0, 0)
+    pack(0, 1, loads[1])
+    send_jump(0, 1)
     empty = jnp.zeros((1, 1, 1) + jump_in.shape[3:], BF16)
     for turn in range(4):
         for h in halves:
             jump_in[pl.ds(turn, 1), pl.ds(h, 1), pl.ds(me, 1)] = empty
-    map_rows = jnp.broadcast_to(map_ref[...].astype(F32), (columns, columns))
+    for copy in loading[3:6]:
+        copy.wait()
+    map_row = map_ref[...].astype(F32)
+    map_row = jnp.concatenate([map_row, jnp.full((1, columns - corners), -1.0, F32)], axis=1)
+    map_rows = jnp.broadcast_to(map_row, (columns, columns))
     map_out[...] = jnp.transpose(map_rows)[:CORNER_PAD]
     map_in[pl.ds(mine, 1)] = map_out[...][None]
     pad = jnp.zeros((CORNER_PAD - corners, chunk), F32)
@@ -191,11 +251,6 @@
         block = coarse_ref[:, g * chunk : (g + 1) * chunk].astype(F32)
         rows_out[g] = jnp.concatenate([block, pad], axis=0).astype(BF16)
 
-    pl.semaphore_wait(barrier, sub_size + grp_size - 2)
-
-    for h in halves:
-        send_jump(0, h)
-
     def send_setup(target):
         remote(map_out, map_in.at[mine], 8, {"grp": target}).start()
         remote(rows_out.at[target], rows_in.at[mine], 9, {"grp": target}).start()
@@ -205,6 +260,21 @@
     couple_pad = jnp.zeros((columns - corners, order), F32)
     couple_full = jnp.concatenate([couple_t_ref[...].astype(F32), couple_pad], axis=0)
     couple[...] = jnp.transpose(couple_full).astype(BF16)
+
+    for copy in loading[6:]:
+        copy.wait()
+    line, _ = split(lax.broadcasted_iota(jnp.int32, (sub_size, total_slots), 1))
+    _, low = split(lax.broadcasted_iota(jnp.int32, (slots, total_slots), 1))
+    spread = lax.broadcasted_iota(jnp.int32, line.shape, 0) == line
+    spread = jnp.where(spread, 1.0, 0.0).astype(BF16)
+    by_slot = [lax.dot_general(d, match, nt, preferred_element_type=F32) for d in digits]
+    row = 32.0 * dot(by_slot[0].astype(BF16), spread) + dot(by_slot[1].astype(BF16), spread)
+    chosen = lax.broadcasted_iota(jnp.int32, row.shape, 0) == low
+    row = jnp.sum(jnp.where(chosen, row, 0.0), axis=0, keepdims=True).astype(jnp.int32) - 1
+    row_sub = lax.broadcasted_iota(jnp.int32, (order, total_slots), 0)
+    place_f = jnp.where(row == row_sub, 1.0, 0.0)
+    place[...] = place_f.astype(BF16)
+    weight = 1.0 - 0.5 * jnp.sum(place_f, axis=1, keepdims=True)
 
     residual, image = [None, None], [None, None]
     for h in halves:
@@ -382,20 +452,14 @@
     loads = subdomain_loads[0, 0]
     couple_t = coupling[0, 0].T
     coarse = coarse_rows[0, 0]
-    neighbor_ids = neighbors[0, 0]
-    row_lists = interface_rows[0, 0]
-    corner_ids = coarse_map[0, 0]
+    neighbor_ids = neighbors[0]
+    row_lists = interface_rows[0, 0].T
+    corner_ids = coarse_map[0]
     order, columns = loads.shape
     corners, coarse_size = coarse.shape
     chunk = coarse_size // grp_size
-    slots = row_lists.shape[1]
+    slots = row_lists.shape[0]
     total_slots = sub_size * slots
-    match = jnp.arange(sub_size, dtype=jnp.int32)[:, None, None] == neighbor_ids[None, :, None]
-    slot_rows = jnp.sum(jnp.where(match, row_lists[None] + 1, 0), axis=1) - 1
-    slot_rows = slot_rows.reshape(sub_size, 2, slots // 2).transpose(1, 0, 2)
-    slot_col = slot_rows.reshape(total_slots, 1)
-    slot_row = slot_rows.reshape(1, total_slots)
-    corner_ids = jnp.pad(corner_ids, (0, columns - corners), constant_values=-1)[None]
     piece = chunk // 2 // z_size
     fold = CORNER_PAD // 2
     vmem = pl.BlockSpec(memory_space=pltpu.VMEM)
@@ -404,14 +468,21 @@
         functools.partial(kernel, x_size),
         name="dual_iteration",
         out_shape=(
-            jax.ShapeDtypeStruct((order, columns), F32),
-            jax.ShapeDtypeStruct((order, columns), F32),
-            jax.ShapeDtypeStruct((1, columns), F32),
+            pltpu.VMEM((order, columns), F32),
+            pltpu.VMEM((order, columns), F32),
+            pltpu.VMEM((1, columns), F32),
         ),
-        in_specs=[vmem, vmem, hbm, vmem, vmem, vmem, vmem, vmem],
+        in_specs=[hbm] * 8,
         out_specs=(vmem, vmem, vmem),
         scratch_shapes=[
+            pltpu.VMEM((order, order), BF16),
+            pltpu.VMEM((order, order), BF16),
             pltpu.VMEM((order, columns), BF16),
+            pltpu.VMEM((corners, order), BF16),
+            pltpu.VMEM((corners, coarse_size), BF16),
+            pltpu.VMEM(neighbor_ids.shape, jnp.int32),
+            pltpu.VMEM(row_lists.shape, jnp.int32),
+            pltpu.VMEM((1, corners), jnp.int32),
             pltpu.VMEM((total_slots, order), BF16),
             pltpu.VMEM((order, total_slots), BF16),
             pltpu.VMEM((order, columns), BF16),
@@ -437,16 +508,16 @@
             pltpu.VMEM((x_size, 8, columns), F32),
             pltpu.VMEM((8, columns), F32),
             pltpu.VMEM((z_size, 8, columns), F32),
-            pltpu.SemaphoreType.DMA,
+            pltpu.SemaphoreType.DMA((8,)),
             pltpu.SemaphoreType.DMA((23,)),
             pltpu.SemaphoreType.DMA((23,)),
         ],
         compiler_params=pltpu.CompilerParams(
             collective_id=0,
             has_side_effects=True,
-            vmem_limit_bytes=48 << 20,
+            vmem_limit_bytes=62 << 20,
         ),
-    )(flex, schur, loads, couple_t, coarse, slot_col, slot_row, corner_ids)
+    )(flex, schur, loads, couple_t, coarse, neighbor_ids, row_lists, corner_ids)
     return ((step * base)[None, None], (base - step * moved)[None, None])
 
 

time: 115 us -> 111 us (0.965)
  local copies, waits for them, and re-layouts: 2.97 us -> 0 us
    unnamed x12 -> x0, local copies, waits for them, and re-layouts: 1.79 us -> none
    pallas_call x1, Pallas kernels: 109 us -> 108 us  [body(): pl.pallas_call(functools.partial(kernel, x_size), name='dual_iteration',...]
where the time goes in v3:
time: 111 us; the launch traced here: 110 us
  Pallas kernels  108 us (97%)
    pallas_call x1, Pallas kernels, body(): pl.pallas_call(functools.partial(kernel, x_size), name='dual_iteration',...  108 us

profile of v3, /device:TPU:1, one launch (start us, length us, event | category | flops | bytes accessed | tf_op | source)
XLA Modules:
  0.0 109.6 jit_solution(4579836479726405492)
XLA Ops:
  0.6 108.2 %dual_iteration.1 = (f32[512,128]{1,0:T(8,128)S(1)}, f32[512,128]{1,0:T(8,128)S(1)}, f32[1,128]{1,0:T(1,128)S(1)}) custom-call(bf16[512,512]{1,0:T(8,128)(2,1)} %bitcast.18, bf16[512,512]{1,0:T(8,128)(2,1)} %bitcast.19, bf16[512,128]{1,0:T(8,128)(2,1)} %bitcast.20, bf16[24,512]{1,0:T(8,128)(2,1)} %bitcast.22, bf16[24,2048]{1,0:T(8,128)(2,1)} %bitcast.21, ...), custom_call_target="tpu_custom_call" | custom-call | tf_op jit(solution)/shard_map/dual_iteration/pallas_call | solution.py:467
  108.8 0.8 subtract_bitcast_fusion
